TPU v7x, 32 devices: a whole 2x2x4 slice. The times are simulated.
32 devices in a mesh: dev: 8 (over z, x), ma: 4 (over y, core).
Axes of the slice: x: 2, y: 2, z: 4, core: 2. Of those that a mesh axis runs over, the one named last changes fastest.
Arguments:
- inputs: bfloat16 [8192, 2048], P('ma', 'dev'), may hold values from -6 to 6
- cotangent: bfloat16 [8192, 2048], P('ma', 'dev'), may hold values from -6 to 6
- factors: bfloat16 [4, 64, 16384], P(None, 'ma', 'dev'), may hold values from -0.5 to 0.5
- exponents: int32 [4, 64], P(None, 'ma'), may hold values from -6 to -4
- error_buffer: bfloat16 [8, 4, 64, 16384], P('dev', None, 'ma'), may hold values from -96 to 96
Outputs:
- output: bfloat16 [8192, 2048], P('ma', 'dev')
- input_grad: bfloat16 [8192, 2048], P('ma', 'dev')
- grad_mean: float32 [4, 64, 16384], P(None, 'ma', 'dev')
- new_error: bfloat16 [8, 4, 64, 16384], P('dev', None, 'ma')
All inputs are finite; a program needn't handle non-finite values.
Results may differ from a plain program's by a relative error of at most 0.0057.
Values may be sent and summed in bfloat16 or wider, within the bound.
A program may use at most 64 MiB of HBM per device.

v0:
```python
import jax
import jax.numpy as jnp
from jax import lax
from jax.sharding import PartitionSpec as P

B = 128
code_limit = 127.0


def regroup(stacked):
    groups = lax.axis_size("ma")
    count, local_blocks, width, tok_count = stacked.shape
    folded = stacked.reshape(
        count, local_blocks, width // (groups * local_blocks), groups, local_blocks, tok_count
    )
    shaped = jnp.transpose(folded, (0, 4, 2, 3, 1, 5))
    arrived = lax.all_to_all(shaped, "ma", split_axis=3, concat_axis=3, tiled=True)
    return arrived.reshape(count, local_blocks, width, tok_count)


def block_forward(weights, values):
    return jnp.einsum("ncd,nct->ndt", weights, values, preferred_element_type=jnp.float32)


def block_backward(weights, values):
    return jnp.einsum("ncd,ndt->nct", weights, values, preferred_element_type=jnp.float32)


def outer_sum(left, right):
    return jnp.einsum("nct,ndt->ncd", left, right, preferred_element_type=jnp.float32)


def quantize(gradients, error_part, exponent_part):
    totals = gradients.reshape(gradients.shape[:-2] + (-1,)) + error_part.astype(jnp.float32)
    scale_inverse = jnp.left_shift(jnp.ones_like(exponent_part), -exponent_part).astype(
        jnp.float32
    )[..., None]
    code_values = jnp.clip(totals * scale_inverse, -code_limit, code_limit)
    return (code_values, (totals - code_values / scale_inverse).astype(jnp.bfloat16), scale_inverse)


def body(inputs, cotangent, factors, exponents, error_buffer):
    local_blocks = factors.shape[1]
    tok_count = inputs.shape[1]
    group_count = lax.axis_size("dev")
    gathered = lax.all_gather(factors, "dev", axis=2, tiled=True)
    matrices = gathered.reshape(gathered.shape[0], local_blocks, B, B)
    block_in = inputs.reshape(local_blocks, B, tok_count)
    block_cot = cotangent.reshape(local_blocks, B, tok_count)
    first_out = block_forward(matrices[0], block_in).astype(jnp.bfloat16)
    mixed_one = regroup(first_out[None])[0]
    second_out = block_forward(matrices[1], mixed_one).astype(jnp.bfloat16)
    pre_gelu = regroup(second_out[None])[0]
    hidden_wide, gelu_back = jax.vjp(jax.nn.gelu, pre_gelu.astype(jnp.float32))
    hidden = hidden_wide.astype(jnp.bfloat16)
    third_out = block_forward(matrices[2], hidden).astype(jnp.bfloat16)
    mixed_two = regroup(third_out[None])[0]
    fourth_out = block_forward(matrices[3], mixed_two).astype(jnp.bfloat16)
    returned = regroup(fourth_out[None])[0]
    output = (block_in.astype(jnp.float32) + returned.astype(jnp.float32)).astype(jnp.bfloat16)
    back_four = regroup(block_cot[None])[0]
    d_mixed_two = block_backward(matrices[3], back_four).astype(jnp.bfloat16)
    gradient_three = outer_sum(mixed_two, back_four)
    d_third = regroup(d_mixed_two[None])[0]
    d_pre = gelu_back(block_backward(matrices[2], d_third))[0].astype(jnp.bfloat16)
    gradient_two = outer_sum(hidden, d_third)
    d_second = regroup(d_pre[None])[0]
    d_mixed_one = block_backward(matrices[1], d_second).astype(jnp.bfloat16)
    gradient_one = outer_sum(mixed_one, d_second)
    d_first = regroup(d_mixed_one[None])[0]
    input_grad = (block_cot.astype(jnp.float32) + block_backward(matrices[0], d_first)).astype(
        jnp.bfloat16
    )
    gradient_zero = outer_sum(block_in, d_first)
    gradients = jnp.stack([gradient_zero, gradient_one, gradient_two, gradient_three])
    code_values, new_part, scale_inverse = quantize(gradients, error_buffer[0], exponents)
    summed = lax.psum_scatter(code_values, "dev", scatter_dimension=2, tiled=True)
    grad_mean = summed / scale_inverse / group_count
    new_error = new_part[None]
    return (
        output.reshape(local_blocks * B, tok_count),
        input_grad.reshape(local_blocks * B, tok_count),
        grad_mean,
        new_error,
    )


def solution(mesh):
    in_specs = (
        P("ma", "dev"),
        P("ma", "dev"),
        P(None, "ma", "dev"),
        P(None, "ma"),
        P("dev", None, "ma", None),
    )
    out_specs = (P("ma", "dev"), P("ma", "dev"), P(None, "ma", "dev"), P("dev", None, "ma", None))
    return jax.shard_map(body, mesh=mesh, in_specs=in_specs, out_specs=out_specs, check_vma=False)
```

profile of v0, /device:TPU:0, one launch (start us, length us, event | category | flops | bytes accessed | tf_op | source)
XLA Modules:
  0.0 293.5 jit_solution(14815720484470332092)
XLA Ops:
  7.9 2.8 copy.67
  10.7 4.3 %all-to-all-start.4 = ((bf16[1,16,2,4,16,256]{5,4,2,1,0,3:T(8,128)(2,1)}), bf16[1,16,2,4,16,256]{5,4,2,1,0,3:T(8,128)(2,1)S(1)}, u32[]{:S(2)}, u32[]{:S(2)}) async-start(bf16[1,16,2,4,16,256]{5,4,2,1,0,3:T(8,128)(2,1)} %copy.67), calls=%async_computation.4 | async-start | bytes 2097152 | tf_op jit(solution)/shard_map/all_to_all | solution.py:17
  14.9 47.0 %all-gather.2.cloned.1.call-done = bf16[4,16,16384]{2,1,0:T(8,128)(2,1)} async-done(((bf16[4,16,2048]{2,1,0:T(8,128)(2,1)}), bf16[4,16,16384]{2,1,0:T(8,128)(2,1)}) %all-gather.2.cloned.1.call-update) | async-done | bytes 2097168 | tf_op jit(solution)/shard_map/all_gather | solution.py:46
  62.0 2.7 slice_bitcast_fusion
  67.2 4.2 %all-to-all-start = ((bf16[1,16,2,4,16,256]{5,1,2,4,0,3:T(8,128)(2,1)}), bf16[1,16,2,4,16,256]{5,1,2,4,0,3:T(8,128)(2,1)}, u32[]{:S(2)}, u32[]{:S(2)}) async-start(bf16[1,16,2,4,16,256]{5,1,2,4,0,3:T(8,128)(2,1)} %bitcast.115), calls=%async_computation | async-start | bytes 2097152 | tf_op jit(solution)/shard_map/all_to_all | solution.py:17
  74.9 11.0 %all-to-all-done = bf16[1,16,2,4,16,256]{5,1,2,4,0,3:T(8,128)(2,1)} async-done(((bf16[1,16,2,4,16,256]{5,1,2,4,0,3:T(8,128)(2,1)}), bf16[1,16,2,4,16,256]{5,1,2,4,0,3:T(8,128)(2,1)}, u32[]{:S(2)}, u32[]{:S(2)}) %all-to-all-start) | async-done | bytes 1048608 | tf_op jit(solution)/shard_map/all_to_all | solution.py:17
  85.9 4.2 %all-to-all-start.5 = ((bf16[1,16,2,4,16,256]{5,1,2,4,0,3:T(8,128)(2,1)}), bf16[1,16,2,4,16,256]{5,1,2,4,0,3:T(8,128)(2,1)}, u32[]{:S(2)}, u32[]{:S(2)}) async-start(bf16[1,16,2,4,16,256]{5,1,2,4,0,3:T(8,128)(2,1)} %bitcast.111), calls=%async_computation.5 | async-start | bytes 2097152 | tf_op jit(solution)/shard_map/all_to_all | solution.py:17
  90.3 2.0 copy.57
  93.9 10.8 %all-to-all-done.5 = bf16[1,16,2,4,16,256]{5,1,2,4,0,3:T(8,128)(2,1)} async-done(((bf16[1,16,2,4,16,256]{5,1,2,4,0,3:T(8,128)(2,1)}), bf16[1,16,2,4,16,256]{5,1,2,4,0,3:T(8,128)(2,1)}, u32[]{:S(2)}, u32[]{:S(2)}) %all-to-all-start.5) | async-done | bytes 1048608 | tf_op jit(solution)/shard_map/all_to_all | solution.py:17
  104.7 4.2 %all-to-all-start.1 = ((bf16[1,16,2,4,16,256]{5,1,2,4,0,3:T(8,128)(2,1)}), bf16[1,16,2,4,16,256]{5,1,2,4,0,3:T(8,128)(2,1)}, u32[]{:S(2)}, u32[]{:S(2)}) async-start(bf16[1,16,2,4,16,256]{5,1,2,4,0,3:T(8,128)(2,1)} %bitcast.138), calls=%async_computation.1 | async-start | bytes 2097152 | tf_op jit(solution)/shard_map/all_to_all | solution.py:17
  108.9 1.9 copy.83
  110.9 2.8 copy.70
  113.6 9.8 %all-to-all-done.1 = bf16[1,16,2,4,16,256]{5,1,2,4,0,3:T(8,128)(2,1)} async-done(((bf16[1,16,2,4,16,256]{5,1,2,4,0,3:T(8,128)(2,1)}), bf16[1,16,2,4,16,256]{5,1,2,4,0,3:T(8,128)(2,1)}, u32[]{:S(2)}, u32[]{:S(2)}) %all-to-all-start.1) | async-done | bytes 1048608 | tf_op jit(solution)/shard_map/all_to_all | solution.py:17
  123.4 2.0 copy.60
  128.1 4.2 %all-to-all-start.6 = ((bf16[1,16,2,4,16,256]{5,1,2,4,0,3:T(8,128)(2,1)}), bf16[1,16,2,4,16,256]{5,1,2,4,0,3:T(8,128)(2,1)}, u32[]{:S(2)}, u32[]{:S(2)}) async-start(bf16[1,16,2,4,16,256]{5,1,2,4,0,3:T(8,128)(2,1)} %bitcast.140), calls=%async_computation.6 | async-start | bytes 2097152 | tf_op jit(solution)/shard_map/all_to_all | solution.py:17
  132.4 2.6 convolution_convert_fusion.3
  136.1 10.8 %all-to-all-done.6 = bf16[1,16,2,4,16,256]{5,1,2,4,0,3:T(8,128)(2,1)} async-done(((bf16[1,16,2,4,16,256]{5,1,2,4,0,3:T(8,128)(2,1)}), bf16[1,16,2,4,16,256]{5,1,2,4,0,3:T(8,128)(2,1)}, u32[]{:S(2)}, u32[]{:S(2)}) %all-to-all-start.6) | async-done | bytes 1048608 | tf_op jit(solution)/shard_map/all_to_all | solution.py:17
  146.8 4.2 %all-to-all-start.2 = ((bf16[1,16,2,4,16,256]{5,1,2,4,0,3:T(8,128)(2,1)}), bf16[1,16,2,4,16,256]{5,1,2,4,0,3:T(8,128)(2,1)}, u32[]{:S(2)}, u32[]{:S(2)}) async-start(bf16[1,16,2,4,16,256]{5,1,2,4,0,3:T(8,128)(2,1)} %bitcast.137), calls=%async_computation.2 | async-start | bytes 2097152 | tf_op jit(solution)/shard_map/all_to_all | solution.py:17
  155.6 10.0 %all-to-all-done.2 = bf16[1,16,2,4,16,256]{5,1,2,4,0,3:T(8,128)(2,1)} async-done(((bf16[1,16,2,4,16,256]{5,1,2,4,0,3:T(8,128)(2,1)}), bf16[1,16,2,4,16,256]{5,1,2,4,0,3:T(8,128)(2,1)}, u32[]{:S(2)}, u32[]{:S(2)}) %all-to-all-start.2) | async-done | bytes 1048608 | tf_op jit(solution)/shard_map/all_to_all | solution.py:17
  165.6 4.2 %all-to-all-start.7 = ((bf16[1,16,2,4,16,256]{5,1,2,4,0,3:T(8,128)(2,1)}), bf16[1,16,2,4,16,256]{5,1,2,4,0,3:T(8,128)(2,1)}, u32[]{:S(2)}, u32[]{:S(2)}) async-start(bf16[1,16,2,4,16,256]{5,1,2,4,0,3:T(8,128)(2,1)} %bitcast.136), calls=%async_computation.7 | async-start | bytes 2097152 | tf_op jit(solution)/shard_map/all_to_all | solution.py:17
  170.1 3.6 %fusion.15 = f32[16,128,128]{2,1,0:T(8,128)} fusion(bf16[16,128,256]{2,1,0:T(8,128)(2,1)} %bitcast.150, f32[16,128,256]{2,1,0:T(8,128)} %bitcast.148), kind=kOutput, calls=%fused_computation.45 | convolution fusion | flops 138936320 | bytes 4194304 | tf_op jit(solution)/shard_map/nct,ndt->ncd/dot_general | solution.py:30
  173.7 2.4 stack.27
  176.1 2.6 fusion.16
  178.8 2.4 stack.26
  192.0 5.4 %fusion.2 = f32[4,16,16384]{2,1,0:T(8,128)} fusion(bf16[1,4,16,16384]{3,2,1,0:T(8,128)(2,1)} %param.9, f32[1,16,16384]{2,1,0:T(8,128)} %stack.28, f32[1,16,16384]{2,1,0:T(8,128)} %stack.27, f32[1,16,16384]{2,1,0:T(8,128)} %stack.26, f32[1,16,16384]{2,1,0:T(8,128)} %stack.25, f32[4,16]{1,0:T(4,128)S(1)} %shift-left_convert_fusion), kind=kLoop, calls=%fused_computation.4 | loop fusion | flops 7340032 | bytes 10486016 | tf_op jit(solution)/shard_map/jit(clip)/min | solution.py:38
  201.2 4.4 %all-to-all-start.3 = ((bf16[1,16,2,4,16,256]{5,1,2,4,0,3:T(8,128)(2,1)}), bf16[1,16,2,4,16,256]{5,1,2,4,0,3:T(8,128)(2,1)}, u32[]{:S(2)}, u32[]{:S(2)}) async-start(bf16[1,16,2,4,16,256]{5,1,2,4,0,3:T(8,128)(2,1)} %bitcast.139), calls=%async_computation.3 | async-start | bytes 2097152 | tf_op jit(solution)/shard_map/all_to_all | solution.py:17
  205.6 2.4 stack.32
  209.2 2.5 stack.33
  212.8 7.2 %all-to-all-done.3 = bf16[1,16,2,4,16,256]{5,1,2,4,0,3:T(8,128)(2,1)} async-done(((bf16[1,16,2,4,16,256]{5,1,2,4,0,3:T(8,128)(2,1)}), bf16[1,16,2,4,16,256]{5,1,2,4,0,3:T(8,128)(2,1)}, u32[]{:S(2)}, u32[]{:S(2)}) %all-to-all-start.3) | async-done | bytes 1048608 | tf_op jit(solution)/shard_map/all_to_all | solution.py:17
  225.9 1.9 subtract_convert_fusion
  227.9 56.8 %reduce-scatter.2.cloned.1.call-done = f32[4,16,2048]{2,1,0:T(8,128)} async-done(((f32[4,16,16384]{2,1,0:T(8,128)}), f32[4,16,2048]{2,1,0:T(8,128)}) %reduce-scatter.2.cloned.1.call-update) | async-done | bytes 524304 | tf_op jit(solution)/shard_map/reduce_scatter | solution.py:77
  284.7 1.9 divide_multiply_fusion
  (87 shorter events, 39.6 us)
Async XLA Ops:
  7.2 54.8 %all-gather.2.cloned.1.call-start = ((), (), s32[]{:S(2)}) async-start(), calls=%async_computation.9 | async-start | bytes 2359296 | tf_op jit(solution)/shard_map/all_gather | solution.py:46
  10.7 56.5 %all-to-all-start.4 = ((bf16[1,16,2,4,16,256]{5,4,2,1,0,3:T(8,128)(2,1)}), bf16[1,16,2,4,16,256]{5,4,2,1,0,3:T(8,128)(2,1)S(1)}, u32[]{:S(2)}, u32[]{:S(2)}) async-start(bf16[1,16,2,4,16,256]{5,4,2,1,0,3:T(8,128)(2,1)} %copy.67), calls=%async_computation.4 | async-start | bytes 2097152 | tf_op jit(solution)/shard_map/all_to_all | solution.py:17
  14.9 50.6 %copy-start = (bf16[2048,256]{1,0:T(8,128)(2,1)S(1)}, bf16[2048,256]{1,0:T(8,128)(2,1)}, u32[]{:S(2)}) copy-start(bf16[2048,256]{1,0:T(8,128)(2,1)} %param.5) | copy-start | bytes 3145732
  67.2 18.7 %all-to-all-start = ((bf16[1,16,2,4,16,256]{5,1,2,4,0,3:T(8,128)(2,1)}), bf16[1,16,2,4,16,256]{5,1,2,4,0,3:T(8,128)(2,1)}, u32[]{:S(2)}, u32[]{:S(2)}) async-start(bf16[1,16,2,4,16,256]{5,1,2,4,0,3:T(8,128)(2,1)} %bitcast.115), calls=%async_computation | async-start | bytes 2097152 | tf_op jit(solution)/shard_map/all_to_all | solution.py:17
  71.4 1.0 copy-start.21
  73.8 16.4 %copy-start.20 = (bf16[2,8,128,128]{3,1,2,0:T(8,128)(2,1)S(1)}, bf16[2,8,128,128]{3,1,2,0:T(8,128)(2,1)}, u32[]{:S(2)}) copy-start(bf16[2,8,128,128]{3,1,2,0:T(8,128)(2,1)} %get-tuple-element.6) | copy-start | bytes 1572868
  85.9 18.7 %all-to-all-start.5 = ((bf16[1,16,2,4,16,256]{5,1,2,4,0,3:T(8,128)(2,1)}), bf16[1,16,2,4,16,256]{5,1,2,4,0,3:T(8,128)(2,1)}, u32[]{:S(2)}, u32[]{:S(2)}) async-start(bf16[1,16,2,4,16,256]{5,1,2,4,0,3:T(8,128)(2,1)} %bitcast.111), calls=%async_computation.5 | async-start | bytes 2097152 | tf_op jit(solution)/shard_map/all_to_all | solution.py:17
  90.3 2.5 copy-start.12
  104.7 18.7 %all-to-all-start.1 = ((bf16[1,16,2,4,16,256]{5,1,2,4,0,3:T(8,128)(2,1)}), bf16[1,16,2,4,16,256]{5,1,2,4,0,3:T(8,128)(2,1)}, u32[]{:S(2)}, u32[]{:S(2)}) async-start(bf16[1,16,2,4,16,256]{5,1,2,4,0,3:T(8,128)(2,1)} %bitcast.138), calls=%async_computation.1 | async-start | bytes 2097152 | tf_op jit(solution)/shard_map/all_to_all | solution.py:17
  123.4 2.0 copy-start.22
  123.4 2.0 copy-start.23
  125.4 1.6 copy-start.19
  128.1 18.7 %all-to-all-start.6 = ((bf16[1,16,2,4,16,256]{5,1,2,4,0,3:T(8,128)(2,1)}), bf16[1,16,2,4,16,256]{5,1,2,4,0,3:T(8,128)(2,1)}, u32[]{:S(2)}, u32[]{:S(2)}) async-start(bf16[1,16,2,4,16,256]{5,1,2,4,0,3:T(8,128)(2,1)} %bitcast.140), calls=%async_computation.6 | async-start | bytes 2097152 | tf_op jit(solution)/shard_map/all_to_all | solution.py:17
  135.0 16.2 %copy-start.24 = (s32[4,16]{1,0:T(4,128)S(1)}, s32[4,16]{1,0:T(4,128)}, u32[]{:S(2)}) copy-start(s32[4,16]{1,0:T(4,128)} %param.8) | copy-start | bytes 772
  146.8 18.7 %all-to-all-start.2 = ((bf16[1,16,2,4,16,256]{5,1,2,4,0,3:T(8,128)(2,1)}), bf16[1,16,2,4,16,256]{5,1,2,4,0,3:T(8,128)(2,1)}, u32[]{:S(2)}, u32[]{:S(2)}) async-start(bf16[1,16,2,4,16,256]{5,1,2,4,0,3:T(8,128)(2,1)} %bitcast.137), calls=%async_computation.2 | async-start | bytes 2097152 | tf_op jit(solution)/shard_map/all_to_all | solution.py:17
  151.1 2.9 copy-start.13
  153.0 1.0 copy-start.5
  165.6 20.1 %all-to-all-start.7 = ((bf16[1,16,2,4,16,256]{5,1,2,4,0,3:T(8,128)(2,1)}), bf16[1,16,2,4,16,256]{5,1,2,4,0,3:T(8,128)(2,1)}, u32[]{:S(2)}, u32[]{:S(2)}) async-start(bf16[1,16,2,4,16,256]{5,1,2,4,0,3:T(8,128)(2,1)} %bitcast.136), calls=%async_computation.7 | async-start | bytes 2097152 | tf_op jit(solution)/shard_map/all_to_all | solution.py:17
  169.9 114.8 %reduce-scatter.2.cloned.1.call-start = ((), (), s32[]{:S(2)}) async-start(), calls=%async_computation.10 | async-start | bytes 4718592 | tf_op jit(solution)/shard_map/reduce_scatter | solution.py:77
  184.4 3.1 %copy-start.2 = (f32[16,128,128]{2,1,0:T(8,128)}, f32[16,128,128]{2,1,0:T(8,128)S(1)}, u32[]{:S(2)}) copy-start(f32[16,128,128]{2,1,0:T(8,128)S(1)} %fusion.17) | copy-start | bytes 3145732
  190.6 6.8 %copy-start.6 = (f32[16,128,128]{2,1,0:T(8,128)}, f32[16,128,128]{2,1,0:T(8,128)S(1)}, u32[]{:S(2)}) copy-start(f32[16,128,128]{2,1,0:T(8,128)S(1)} %copy.75) | copy-start | bytes 3145732
  197.3 1.2 copy-start.4
  201.2 6.8 %copy-start.1 = (f32[16,128,128]{2,1,0:T(8,128)S(1)}, f32[16,128,128]{2,1,0:T(8,128)}, u32[]{:S(2)}) copy-start(f32[16,128,128]{2,1,0:T(8,128)} %fusion.16) | copy-start | bytes 3145732
  201.2 18.9 %all-to-all-start.3 = ((bf16[1,16,2,4,16,256]{5,1,2,4,0,3:T(8,128)(2,1)}), bf16[1,16,2,4,16,256]{5,1,2,4,0,3:T(8,128)(2,1)}, u32[]{:S(2)}, u32[]{:S(2)}) async-start(bf16[1,16,2,4,16,256]{5,1,2,4,0,3:T(8,128)(2,1)} %bitcast.139), calls=%async_computation.3 | async-start | bytes 2097152 | tf_op jit(solution)/shard_map/all_to_all | solution.py:17
  209.2 2.5 copy-start.7
  212.8 9.2 %copy-start.10 = (bf16[2,8,128,128]{3,2,1,0:T(8,128)(2,1)S(1)}, bf16[2,8,128,128]{3,2,1,0:T(8,128)(2,1)}, u32[]{:S(2)}) copy-start(bf16[2,8,128,128]{3,2,1,0:T(8,128)(2,1)} %copy-done.9) | copy-start | bytes 1572868
  220.1 1.9 copy-start.14
  222.0 2.7 copy-start.16
  222.0 2.7 copy-start.17
  222.0 2.7 copy-start.18
  223.5 2.2 copy-start.8
  223.5 2.5 copy-start.15
  (3 other events, 2.6 us)
Sparse Core Ops, SparseCore 0:
  10.2 51.7 all-gather.1
  197.5 87.1 reduce-scatter.1
where the time goes:
time: 295 us; the launch traced here: 293 us
  waiting for transfers between devices  164 us (56%)
  local copies, waits for them, and re-layouts  52.9 us (18%)
  starting transfers between devices  34.4 us (12%)
  matrix products  17.1 us (6%)
  between operations  14.4 us (5%)
  other arithmetic  10.6 us (4%)
    all_to_all x8, waiting for transfers between devices, regroup(): lax.all_to_all(shaped, 'ma', split_axis=3, concat_axis=3, tiled=True)  59.6 us
    reduce_scatter x1, waiting for transfers between devices, body(): lax.psum_scatter(code_values, 'dev', scatter_dimension=2, tiled=True)  56.8 us
    all_gather x1, waiting for transfers between devices, body(): gathered = lax.all_gather(factors, 'dev', axis=2, tiled=True)  47 us
    all_to_all x8, starting transfers between devices, regroup(): lax.all_to_all(shaped, 'ma', split_axis=3, concat_axis=3, tiled=True)  34.1 us
    another operation x8, local copies, waits for them, and re-layouts, body(): jnp.stack([gradient_zero, gradient_one, gradient_two, gradient_three])  14.7 us
    all_to_all x7, local copies, waits for them, and re-layouts, regroup(): lax.all_to_all(shaped, 'ma', split_axis=3, concat_axis=3, tiled=True)  12.3 us
    unnamed x55, local copies, waits for them, and re-layouts  11.8 us
    dot_general x4, matrix products, outer_sum(): jnp.einsum('nct,ndt->ncd', left, right, preferred_element_type=jnp.float32)  8.22 us
  transfers between devices with their start and end apart: 10, of which 8 were waited for; matrix products, arithmetic and copies ran while one was open for 19% of the time, Pallas kernels for 0%

commit v1 on v0

--- a/solution.py
+++ b/solution.py
@@ -7,6 +7,18 @@
 code_limit = 127.0
 
 
+def cut_along(x, dim, size):
+    dims = x.shape
+    parts = x.reshape(*dims[:dim], size, dims[dim] // size, *dims[dim + 1 :])
+    return jnp.moveaxis(parts, dim, 0)
+
+
+def joined_along(blocks, dim):
+    shape = list(blocks.shape[1:])
+    shape[dim] *= blocks.shape[0]
+    return jnp.moveaxis(blocks, 0, dim).reshape(shape)
+
+
 def regroup(stacked):
     groups = lax.axis_size("ma")
     count, local_blocks, width, tok_count = stacked.shape
@@ -14,7 +26,14 @@
         count, local_blocks, width // (groups * local_blocks), groups, local_blocks, tok_count
     )
     shaped = jnp.transpose(folded, (0, 4, 2, 3, 1, 5))
-    arrived = lax.all_to_all(shaped, "ma", split_axis=3, concat_axis=3, tiled=True)
+    devices, position = (lax.axis_size("ma"), lax.axis_index("ma"))
+    blocks = cut_along(shaped, 3, devices)
+    gathered_2 = [blocks[position]]
+    for hop in range(1, devices):
+        sent = blocks[position ^ hop]
+        gathered_2.append(lax.ppermute(sent, "ma", [(i, i ^ hop) for i in range(devices)]))
+    blocks = jnp.stack(gathered_2)[position ^ jnp.arange(devices)]
+    arrived = joined_along(blocks, 3)
     return arrived.reshape(count, local_blocks, width, tok_count)
 
 

time: 295 us -> 274 us (0.929)
  starting transfers between devices: 34.4 us -> 18.3 us
  waiting for transfers between devices: 164 us -> 152 us
  other arithmetic: 10.6 us -> 20.8 us
  matrix products: 17.1 us -> 11.8 us
    all_to_all x8 -> x0, waiting for transfers between devices: 59.6 us -> none  [regroup(): lax.all_to_all(shaped, 'ma', split_axis=3, concat_axis=3, tiled=True)]
    ppermute x0 -> x24, waiting for transfers between devices: none -> 55.8 us  [regroup(): lax.ppermute(sent, 'ma', [(i, i ^ hop) for i in range(devices)])]
    all_to_all x8 -> x0, starting transfers between devices: 34.1 us -> none  [regroup(): lax.all_to_all(shaped, 'ma', split_axis=3, concat_axis=3, tiled=True)]
    ppermute x0 -> x24, starting transfers between devices: none -> 18.3 us  [regroup(): lax.ppermute(sent, 'ma', [(i, i ^ hop) for i in range(devices)])]
    all_to_all x7 -> x0, local copies, waits for them, and re-layouts: 12.3 us -> none  [regroup(): lax.all_to_all(shaped, 'ma', split_axis=3, concat_axis=3, tiled=True)]
    gather x0 -> x8, local copies, waits for them, and re-layouts: none -> 12.2 us  [regroup(): blocks = jnp.stack(gathered_2)[position ^ jnp.arange(devices)]]
    all_gather x1, waiting for transfers between devices: 47 us -> 35.7 us  [body(): gathered = lax.all_gather(factors, 'dev', axis=2, tiled=True)]
    another operation x0 -> x8, other arithmetic: none -> 9.72 us  [regroup(): blocks = jnp.stack(gathered_2)[position ^ jnp.arange(devices)]]
  transfers between devices with their start and end apart: 10 -> 26, of which waited for: 8 -> 13; matrix products, arithmetic and copies ran while one was open for 19% -> 17% of each run, Pallas kernels for 0% -> 0%
where the time goes in v1:
time: 274 us; the launch traced here: 273 us
  waiting for transfers between devices  152 us (55%)
  local copies, waits for them, and re-layouts  55.4 us (20%)
  other arithmetic  20.8 us (8%)
  starting transfers between devices  18.3 us (7%)
  between operations  14.5 us (5%)
  matrix products  11.8 us (4%)
    reduce_scatter x1, waiting for transfers between devices, body(): lax.psum_scatter(code_values, 'dev', scatter_dimension=2, tiled=True)  60 us
    ppermute x24, waiting for transfers between devices, regroup(): lax.ppermute(sent, 'ma', [(i, i ^ hop) for i in range(devices)])  55.8 us
    all_gather x1, waiting for transfers between devices, body(): gathered = lax.all_gather(factors, 'dev', axis=2, tiled=True)  35.7 us
    ppermute x24, starting transfers between devices, regroup(): lax.ppermute(sent, 'ma', [(i, i ^ hop) for i in range(devices)])  18.3 us
    another operation x8, local copies, waits for them, and re-layouts, body(): jnp.stack([gradient_zero, gradient_one, gradient_two, gradient_three])  12.3 us
    gather x8, local copies, waits for them, and re-layouts, regroup(): blocks = jnp.stack(gathered_2)[position ^ jnp.arange(devices)]  12.2 us
    transpose x6, local copies, waits for them, and re-layouts, joined_along(): return jnp.moveaxis(blocks, 0, dim).reshape(shape)  11.8 us
    another operation x8, other arithmetic, regroup(): blocks = jnp.stack(gathered_2)[position ^ jnp.arange(devices)]  9.72 us
  transfers between devices with their start and end apart: 26, of which 13 were waited for; matrix products, arithmetic and copies ran while one was open for 17% of the time, Pallas kernels for 0%

profile of v1, /device:TPU:0, one launch (start us, length us, event | category | flops | bytes accessed | tf_op | source)
XLA Modules:
  0.0 273.0 jit_solution(2564828168525342323)
XLA Ops:
  9.8 2.6 collective-permute-start.14
  12.5 6.6 %collective-permute-done.14 = bf16[1,16,2,1,16,256]{5,1,3,2,4,0:T(8,128)(2,1)S(1)} collective-permute-done((bf16[1,16,2,1,16,256]{5,1,3,2,4,0:T(8,128)(2,1)S(1)}, bf16[1,16,2,1,16,256]{5,1,3,2,4,0:T(8,128)(2,1)S(1)}, u32[]{:S(2)}, u32[]{:S(2)}) %collective-permute-start.14) | collective-permute-done | bytes 262176 | tf_op jit(solution)/shard_map/ppermute | solution.py:34
  19.1 5.8 %collective-permute-done.13 = bf16[1,16,2,1,16,256]{5,1,2,4,3,0:T(8,128)(2,1)S(1)} collective-permute-done((bf16[1,16,2,1,16,256]{5,1,2,4,3,0:T(8,128)(2,1)S(1)}, bf16[1,16,2,1,16,256]{5,1,2,4,3,0:T(8,128)(2,1)S(1)}, u32[]{:S(2)}, u32[]{:S(2)}) %collective-permute-start.13) | collective-permute-done | bytes 262176 | tf_op jit(solution)/shard_map/ppermute | solution.py:34
  26.3 35.7 %all-gather.2.cloned.1.call-done = bf16[4,16,16384]{2,1,0:T(8,128)(2,1)} async-done(((bf16[4,16,2048]{2,1,0:T(8,128)(2,1)}), bf16[4,16,16384]{2,1,0:T(8,128)(2,1)}) %all-gather.2.cloned.1.call-update) | async-done | bytes 2097168 | tf_op jit(solution)/shard_map/all_gather | solution.py:65
  62.0 1.7 slice_bitcast_fusion
  71.8 2.4 collective-permute-done.2
  74.2 6.6 %collective-permute-done.1 = bf16[1,16,2,1,16,256]{5,1,2,4,3,0:T(8,128)(2,1)S(1)} collective-permute-done((bf16[1,16,2,1,16,256]{5,1,2,4,3,0:T(8,128)(2,1)S(1)}, bf16[1,16,2,1,16,256]{5,1,2,4,3,0:T(8,128)(2,1)S(1)}, u32[]{:S(2)}, u32[]{:S(2)}) %collective-permute-start.1) | collective-permute-done | bytes 262176 | tf_op jit(solution)/shard_map/ppermute | solution.py:34
  82.6 1.8 copy.49
  89.0 3.2 %collective-permute-done.16 = bf16[1,16,2,1,16,256]{5,1,2,4,3,0:T(8,128)(2,1)} collective-permute-done((bf16[1,16,2,1,16,256]{5,1,2,4,3,0:T(8,128)(2,1)}, bf16[1,16,2,1,16,256]{5,1,2,4,3,0:T(8,128)(2,1)}, u32[]{:S(2)}, u32[]{:S(2)}) %collective-permute-start.16) | collective-permute-done | bytes 262176 | tf_op jit(solution)/shard_map/ppermute | solution.py:34
  95.0 2.8 %copy.72 = bf16[1,16,2,4,1,16,256]{6,5,3,2,1,4,0:T(8,128)(2,1)} copy(bf16[1,16,2,4,1,16,256]{6,1,2,5,3,4,0:T(8,128)(2,1)} %bitcast.321) | data formatting | bytes 2097152 | tf_op jit(solution)/shard_map/transpose | solution.py:19
  97.8 5.0 %collective-permute-done.4 = bf16[1,16,2,1,16,256]{5,1,2,4,3,0:T(8,128)(2,1)} collective-permute-done((bf16[1,16,2,1,16,256]{5,1,2,4,3,0:T(8,128)(2,1)}, bf16[1,16,2,1,16,256]{5,1,2,4,3,0:T(8,128)(2,1)}, u32[]{:S(2)}, u32[]{:S(2)}) %collective-permute-start.4) | collective-permute-done | bytes 262176 | tf_op jit(solution)/shard_map/ppermute | solution.py:34
  102.8 2.2 maximum_bitcast_fusion.1
  105.0 1.8 gather_fusion.1
  119.2 5.2 %collective-permute-done.20 = bf16[1,16,2,1,16,256]{5,1,3,2,4,0:T(8,128)(2,1)} collective-permute-done((bf16[1,16,2,1,16,256]{5,1,3,2,4,0:T(8,128)(2,1)}, bf16[1,16,2,1,16,256]{5,1,3,2,4,0:T(8,128)(2,1)}, u32[]{:S(2)}, u32[]{:S(2)}) %collective-permute-start.20) | collective-permute-done | bytes 262176 | tf_op jit(solution)/shard_map/ppermute | solution.py:34
  124.5 6.6 %collective-permute-done.19 = bf16[1,16,2,1,16,256]{5,1,2,4,3,0:T(8,128)(2,1)} collective-permute-done((bf16[1,16,2,1,16,256]{5,1,2,4,3,0:T(8,128)(2,1)}, bf16[1,16,2,1,16,256]{5,1,2,4,3,0:T(8,128)(2,1)}, u32[]{:S(2)}, u32[]{:S(2)}) %collective-permute-start.19) | collective-permute-done | bytes 262176 | tf_op jit(solution)/shard_map/ppermute | solution.py:34
  134.0 2.0 copy.76
  137.5 2.2 maximum_bitcast_fusion.2
  139.7 2.8 %gather_fusion.2 = bf16[4,16,2,16,256]{4,1,2,3,0:T(8,128)(2,1)} fusion(bf16[4,16,2,16,256]{4,1,2,3,0:T(8,128)(2,1)} %maximum_bitcast_fusion.2, s32[1024]{0:T(1024)S(1)} %pad_clamp_fusion), kind=kCustom, calls=%fused_computation.2 | custom fusion | bytes 2097168 | tf_op jit(solution)/shard_map/gather | solution.py:35
  142.5 2.8 %copy.59 = bf16[1,16,2,4,1,16,256]{6,5,3,2,1,4,0:T(8,128)(2,1)} copy(bf16[1,16,2,4,1,16,256]{6,1,2,5,3,4,0:T(8,128)(2,1)} %bitcast.323) | data formatting | bytes 2097152 | tf_op jit(solution)/shard_map/transpose | solution.py:19
  149.6 1.7 fusion.18
  152.4 2.4 collective-permute-done.23
  154.8 5.9 %collective-permute-done.22 = bf16[1,16,2,1,16,256]{5,1,2,4,3,0:T(8,128)(2,1)} collective-permute-done((bf16[1,16,2,1,16,256]{5,1,2,4,3,0:T(8,128)(2,1)}, bf16[1,16,2,1,16,256]{5,1,2,4,3,0:T(8,128)(2,1)}, u32[]{:S(2)}, u32[]{:S(2)}) %collective-permute-start.22) | collective-permute-done | bytes 262176 | tf_op jit(solution)/shard_map/ppermute | solution.py:34
  163.6 1.9 copy.80
  166.9 2.5 copy.81
  169.4 2.4 stack.153
  171.8 5.4 %fusion.2 = f32[4,16,16384]{2,1,0:T(8,128)} fusion(bf16[1,4,16,16384]{3,2,1,0:T(8,128)(2,1)} %param.9, f32[1,16,16384]{2,1,0:T(8,128)} %stack.156, f32[1,16,16384]{2,1,0:T(8,128)} %stack.155, f32[1,16,16384]{2,1,0:T(8,128)} %stack.154, f32[1,16,16384]{2,1,0:T(8,128)} %stack.153, f32[4,16]{1,0:T(4,128)S(1)} %shift-left_convert_fusion), kind=kLoop, calls=%fused_computation.12 | loop fusion | flops 7340032 | bytes 10486016 | tf_op jit(solution)/shard_map/jit(clip)/min | solution.py:57
  177.2 1.8 convolution_convert_fusion.2
  182.1 2.6 stack.160
  188.6 5.9 %collective-permute-done.10 = bf16[1,16,2,1,16,256]{5,1,2,4,3,0:T(8,128)(2,1)} collective-permute-done((bf16[1,16,2,1,16,256]{5,1,2,4,3,0:T(8,128)(2,1)}, bf16[1,16,2,1,16,256]{5,1,2,4,3,0:T(8,128)(2,1)}, u32[]{:S(2)}, u32[]{:S(2)}) %collective-permute-start.10) | collective-permute-done | bytes 262176 | tf_op jit(solution)/shard_map/ppermute | solution.py:34
  202.3 2.0 subtract_convert_fusion
  204.3 60.0 %reduce-scatter.2.cloned.1.call-done = f32[4,16,2048]{2,1,0:T(8,128)} async-done(((f32[4,16,16384]{2,1,0:T(8,128)}), f32[4,16,2048]{2,1,0:T(8,128)}) %reduce-scatter.2.cloned.1.call-update) | async-done | bytes 524304 | tf_op jit(solution)/shard_map/reduce_scatter | solution.py:96
  264.2 1.9 divide_multiply_fusion
  (129 shorter events, 62.2 us)
Async XLA Ops:
  7.2 54.8 %all-gather.2.cloned.1.call-start = ((), (), s32[]{:S(2)}) async-start(), calls=%async_computation.1 | async-start | bytes 2359296 | tf_op jit(solution)/shard_map/all_gather | solution.py:65
  7.9 256.3 %reduce-scatter.2.cloned.1.call-start = ((), (), s32[]{:S(2)}) async-start(), calls=%async_computation.2 | async-start | bytes 4718592 | tf_op jit(solution)/shard_map/reduce_scatter | solution.py:96
  9.3 3.2 %collective-permute-start.12 = (bf16[1,16,2,1,16,256]{5,1,2,4,3,0:T(8,128)(2,1)S(1)}, bf16[1,16,2,1,16,256]{5,1,2,4,3,0:T(8,128)(2,1)S(1)}, u32[]{:S(2)}, u32[]{:S(2)}) collective-permute-start(bf16[1,16,2,1,16,256]{5,1,2,4,3,0:T(8,128)(2,1)S(1)} %get-tuple-element.21), channel_id=1, source_target_pairs={{0,1},{1,0},{2,3},{3,2},{4,5},{5,4},{6,7},{7,6},{8,9},{9,8},{10,11... | collective-permute-start | bytes 786440 | tf_op jit(solution)/shard_map/ppermute | solution.py:34
  9.8 9.3 %collective-permute-start.14 = (bf16[1,16,2,1,16,256]{5,1,3,2,4,0:T(8,128)(2,1)S(1)}, bf16[1,16,2,1,16,256]{5,1,3,2,4,0:T(8,128)(2,1)S(1)}, u32[]{:S(2)}, u32[]{:S(2)}) collective-permute-start(bf16[1,16,2,1,16,256]{5,1,3,2,4,0:T(8,128)(2,1)S(1)} %get-tuple-element.22), channel_id=1, source_target_pairs={{0,3},{1,2},{2,1},{3,0},{4,7},{5,6},{6,5},{7,4},{8,11},{9,10},{10,... | collective-permute-start | bytes 786440 | tf_op jit(solution)/shard_map/ppermute | solution.py:34
  12.4 12.5 %collective-permute-start.13 = (bf16[1,16,2,1,16,256]{5,1,2,4,3,0:T(8,128)(2,1)S(1)}, bf16[1,16,2,1,16,256]{5,1,2,4,3,0:T(8,128)(2,1)S(1)}, u32[]{:S(2)}, u32[]{:S(2)}) collective-permute-start(bf16[1,16,2,1,16,256]{5,1,2,4,3,0:T(8,128)(2,1)S(1)} %get-tuple-element.23), channel_id=1, source_target_pairs={{0,2},{1,3},{2,0},{3,1},{4,6},{5,7},{6,4},{7,5},{8,10},{9,11},{10,... | collective-permute-start | bytes 786440 | tf_op jit(solution)/shard_map/ppermute | solution.py:34
  63.7 4.3 %copy-start.7 = (bf16[2,8,128,128]{3,2,1,0:T(8,128)(2,1)}, bf16[2,8,128,128]{3,2,1,0:T(8,128)(2,1)S(1)}, u32[]{:S(2)}) copy-start(bf16[2,8,128,128]{3,2,1,0:T(8,128)(2,1)S(1)} %copy.114) | copy-start | bytes 1572868
  65.9 5.4 %collective-permute-start = (bf16[1,16,2,1,16,256]{5,1,2,4,3,0:T(8,128)(2,1)S(1)}, bf16[1,16,2,1,16,256]{5,1,2,4,3,0:T(8,128)(2,1)S(1)}, u32[]{:S(2)}, u32[]{:S(2)}) collective-permute-start(bf16[1,16,2,1,16,256]{5,1,2,4,3,0:T(8,128)(2,1)S(1)} %get-tuple-element.37), channel_id=1, source_target_pairs={{0,1},{1,0},{2,3},{3,2},{4,5},{5,4},{6,7},{7,6},{8,9},{9,8},{10,11... | collective-permute-start | bytes 786440 | tf_op jit(solution)/shard_map/ppermute | solution.py:34
  65.9 8.3 %collective-permute-start.2 = (bf16[1,16,2,1,16,256]{5,1,3,2,4,0:T(8,128)(2,1)S(1)}, bf16[1,16,2,1,16,256]{5,1,3,2,4,0:T(8,128)(2,1)S(1)}, u32[]{:S(2)}, u32[]{:S(2)}) collective-permute-start(bf16[1,16,2,1,16,256]{5,1,3,2,4,0:T(8,128)(2,1)S(1)} %get-tuple-element.38), channel_id=1, source_target_pairs={{0,3},{1,2},{2,1},{3,0},{4,7},{5,6},{6,5},{7,4},{8,11},{9,10},{10,... | collective-permute-start | bytes 786440 | tf_op jit(solution)/shard_map/ppermute | solution.py:34
  67.5 13.3 %collective-permute-start.1 = (bf16[1,16,2,1,16,256]{5,1,2,4,3,0:T(8,128)(2,1)S(1)}, bf16[1,16,2,1,16,256]{5,1,2,4,3,0:T(8,128)(2,1)S(1)}, u32[]{:S(2)}, u32[]{:S(2)}) collective-permute-start(bf16[1,16,2,1,16,256]{5,1,2,4,3,0:T(8,128)(2,1)S(1)} %get-tuple-element.39), channel_id=1, source_target_pairs={{0,2},{1,3},{2,0},{3,1},{4,6},{5,7},{6,4},{7,5},{8,10},{9,11},{10,... | collective-permute-start | bytes 786440 | tf_op jit(solution)/shard_map/ppermute | solution.py:34
  68.6 15.8 %copy-start.8 = (bf16[2,8,128,128]{3,2,1,0:T(8,128)(2,1)}, bf16[2,8,128,128]{3,2,1,0:T(8,128)(2,1)S(1)}, u32[]{:S(2)}) copy-start(bf16[2,8,128,128]{3,2,1,0:T(8,128)(2,1)S(1)} %copy.112) | copy-start | bytes 1572868
  69.6 17.9 %collective-permute-start.15 = (bf16[1,16,2,1,16,256]{5,1,2,4,3,0:T(8,128)(2,1)}, bf16[1,16,2,1,16,256]{5,1,2,4,3,0:T(8,128)(2,1)}, u32[]{:S(2)}, u32[]{:S(2)}) collective-permute-start(bf16[1,16,2,1,16,256]{5,1,2,4,3,0:T(8,128)(2,1)} %get-tuple-element.17), channel_id=1, source_target_pairs={{0,1},{1,0},{2,3},{3,2},{4,5},{5,4},{6,7},{7,6},{8,9},{9,8},{10,11... | collective-permute-start | bytes 786440 | tf_op jit(solution)/shard_map/ppermute | solution.py:34
  69.6 19.3 %collective-permute-start.17 = (bf16[1,16,2,1,16,256]{5,1,3,2,4,0:T(8,128)(2,1)}, bf16[1,16,2,1,16,256]{5,1,3,2,4,0:T(8,128)(2,1)}, u32[]{:S(2)}, u32[]{:S(2)}) collective-permute-start(bf16[1,16,2,1,16,256]{5,1,3,2,4,0:T(8,128)(2,1)} %get-tuple-element.18), channel_id=1, source_target_pairs={{0,3},{1,2},{2,1},{3,0},{4,7},{5,6},{6,5},{7,4},{8,11},{9,10},{10,... | collective-permute-start | bytes 786440 | tf_op jit(solution)/shard_map/ppermute | solution.py:34
  71.2 20.9 %collective-permute-start.16 = (bf16[1,16,2,1,16,256]{5,1,2,4,3,0:T(8,128)(2,1)}, bf16[1,16,2,1,16,256]{5,1,2,4,3,0:T(8,128)(2,1)}, u32[]{:S(2)}, u32[]{:S(2)}) collective-permute-start(bf16[1,16,2,1,16,256]{5,1,2,4,3,0:T(8,128)(2,1)} %get-tuple-element.19), channel_id=1, source_target_pairs={{0,2},{1,3},{2,0},{3,1},{4,6},{5,7},{6,4},{7,5},{8,10},{9,11},{10,... | collective-permute-start | bytes 786440 | tf_op jit(solution)/shard_map/ppermute | solution.py:34
  84.4 3.7 %copy-start.19 = (s32[4,16]{1,0:T(4,128)S(1)}, s32[4,16]{1,0:T(4,128)}, u32[]{:S(2)}) copy-start(s32[4,16]{1,0:T(4,128)} %param.8) | copy-start | bytes 772
  85.9 11.9 %collective-permute-start.3 = (bf16[1,16,2,1,16,256]{5,1,2,4,3,0:T(8,128)(2,1)}, bf16[1,16,2,1,16,256]{5,1,2,4,3,0:T(8,128)(2,1)}, u32[]{:S(2)}, u32[]{:S(2)}) collective-permute-start(bf16[1,16,2,1,16,256]{5,1,2,4,3,0:T(8,128)(2,1)} %get-tuple-element.33), channel_id=1, source_target_pairs={{0,1},{1,0},{2,3},{3,2},{4,5},{5,4},{6,7},{7,6},{8,9},{9,8},{10,11... | collective-permute-start | bytes 786440 | tf_op jit(solution)/shard_map/ppermute | solution.py:34
  85.9 11.9 %collective-permute-start.5 = (bf16[1,16,2,1,16,256]{5,1,3,2,4,0:T(8,128)(2,1)}, bf16[1,16,2,1,16,256]{5,1,3,2,4,0:T(8,128)(2,1)}, u32[]{:S(2)}, u32[]{:S(2)}) collective-permute-start(bf16[1,16,2,1,16,256]{5,1,3,2,4,0:T(8,128)(2,1)} %get-tuple-element.34), channel_id=1, source_target_pairs={{0,3},{1,2},{2,1},{3,0},{4,7},{5,6},{6,5},{7,4},{8,11},{9,10},{10,... | collective-permute-start | bytes 786440 | tf_op jit(solution)/shard_map/ppermute | solution.py:34
  87.5 15.3 %collective-permute-start.4 = (bf16[1,16,2,1,16,256]{5,1,2,4,3,0:T(8,128)(2,1)}, bf16[1,16,2,1,16,256]{5,1,2,4,3,0:T(8,128)(2,1)}, u32[]{:S(2)}, u32[]{:S(2)}) collective-permute-start(bf16[1,16,2,1,16,256]{5,1,2,4,3,0:T(8,128)(2,1)} %get-tuple-element.35), channel_id=1, source_target_pairs={{0,2},{1,3},{2,0},{3,1},{4,6},{5,7},{6,4},{7,5},{8,10},{9,11},{10,... | collective-permute-start | bytes 786440 | tf_op jit(solution)/shard_map/ppermute | solution.py:34
  93.4 9.4 %copy-start.17 = (bf16[1,1,16,2,1,16,256]{6,2,3,5,4,1,0:T(8,128)(2,1)S(1)}, bf16[1,1,16,2,1,16,256]{6,2,3,5,4,1,0:T(8,128)(2,1)}, u32[]{:S(2)}) copy-start(bf16[1,1,16,2,1,16,256]{6,2,3,5,4,1,0:T(8,128)(2,1)} %get-tuple-element.32) | copy-start | bytes 786436
  110.2 27.2 %collective-permute-start.6 = (bf16[1,16,2,1,16,256]{5,1,2,4,3,0:T(8,128)(2,1)}, bf16[1,16,2,1,16,256]{5,1,2,4,3,0:T(8,128)(2,1)}, u32[]{:S(2)}, u32[]{:S(2)}) collective-permute-start(bf16[1,16,2,1,16,256]{5,1,2,4,3,0:T(8,128)(2,1)} %get-tuple-element.29), channel_id=1, source_target_pairs={{0,1},{1,0},{2,3},{3,2},{4,5},{5,4},{6,7},{7,6},{8,9},{9,8},{10,11... | collective-permute-start | bytes 786440 | tf_op jit(solution)/shard_map/ppermute | solution.py:34
  110.2 27.2 %collective-permute-start.8 = (bf16[1,16,2,1,16,256]{5,1,3,2,4,0:T(8,128)(2,1)}, bf16[1,16,2,1,16,256]{5,1,3,2,4,0:T(8,128)(2,1)}, u32[]{:S(2)}, u32[]{:S(2)}) collective-permute-start(bf16[1,16,2,1,16,256]{5,1,3,2,4,0:T(8,128)(2,1)} %get-tuple-element.30), channel_id=1, source_target_pairs={{0,3},{1,2},{2,1},{3,0},{4,7},{5,6},{6,5},{7,4},{8,11},{9,10},{10,... | collective-permute-start | bytes 786440 | tf_op jit(solution)/shard_map/ppermute | solution.py:34
  114.4 4.3 %collective-permute-start.18 = (bf16[1,16,2,1,16,256]{5,1,2,4,3,0:T(8,128)(2,1)}, bf16[1,16,2,1,16,256]{5,1,2,4,3,0:T(8,128)(2,1)}, u32[]{:S(2)}, u32[]{:S(2)}) collective-permute-start(bf16[1,16,2,1,16,256]{5,1,2,4,3,0:T(8,128)(2,1)} %get-tuple-element.13), channel_id=1, source_target_pairs={{0,1},{1,0},{2,3},{3,2},{4,5},{5,4},{6,7},{7,6},{8,9},{9,8},{10,11... | collective-permute-start | bytes 786440 | tf_op jit(solution)/shard_map/ppermute | solution.py:34
  114.4 10.1 %collective-permute-start.20 = (bf16[1,16,2,1,16,256]{5,1,3,2,4,0:T(8,128)(2,1)}, bf16[1,16,2,1,16,256]{5,1,3,2,4,0:T(8,128)(2,1)}, u32[]{:S(2)}, u32[]{:S(2)}) collective-permute-start(bf16[1,16,2,1,16,256]{5,1,3,2,4,0:T(8,128)(2,1)} %get-tuple-element.14), channel_id=1, source_target_pairs={{0,3},{1,2},{2,1},{3,0},{4,7},{5,6},{6,5},{7,4},{8,11},{9,10},{10,... | collective-permute-start | bytes 786440 | tf_op jit(solution)/shard_map/ppermute | solution.py:34
  115.1 16.0 %collective-permute-start.19 = (bf16[1,16,2,1,16,256]{5,1,2,4,3,0:T(8,128)(2,1)}, bf16[1,16,2,1,16,256]{5,1,2,4,3,0:T(8,128)(2,1)}, u32[]{:S(2)}, u32[]{:S(2)}) collective-permute-start(bf16[1,16,2,1,16,256]{5,1,2,4,3,0:T(8,128)(2,1)} %get-tuple-element.15), channel_id=1, source_target_pairs={{0,2},{1,3},{2,0},{3,1},{4,6},{5,7},{6,4},{7,5},{8,10},{9,11},{10,... | collective-permute-start | bytes 786440 | tf_op jit(solution)/shard_map/ppermute | solution.py:34
  117.3 13.8 %copy-start.15 = (f32[16,128,128]{2,1,0:T(8,128)}, f32[16,128,128]{2,1,0:T(8,128)S(1)}, u32[]{:S(2)}) copy-start(f32[16,128,128]{2,1,0:T(8,128)S(1)} %fusion.16) | copy-start | bytes 3145732
  118.7 18.8 %collective-permute-start.7 = (bf16[1,16,2,1,16,256]{5,1,2,4,3,0:T(8,128)(2,1)}, bf16[1,16,2,1,16,256]{5,1,2,4,3,0:T(8,128)(2,1)}, u32[]{:S(2)}, u32[]{:S(2)}) collective-permute-start(bf16[1,16,2,1,16,256]{5,1,2,4,3,0:T(8,128)(2,1)} %get-tuple-element.31), channel_id=1, source_target_pairs={{0,2},{1,3},{2,0},{3,1},{4,6},{5,7},{6,4},{7,5},{8,10},{9,11},{10,... | collective-permute-start | bytes 786440 | tf_op jit(solution)/shard_map/ppermute | solution.py:34
  146.2 6.2 %collective-permute-start.21 = (bf16[1,16,2,1,16,256]{5,1,2,4,3,0:T(8,128)(2,1)}, bf16[1,16,2,1,16,256]{5,1,2,4,3,0:T(8,128)(2,1)}, u32[]{:S(2)}, u32[]{:S(2)}) collective-permute-start(bf16[1,16,2,1,16,256]{5,1,2,4,3,0:T(8,128)(2,1)} %get-tuple-element.9), channel_id=1, source_target_pairs={{0,1},{1,0},{2,3},{3,2},{4,5},{5,4},{6,7},{7,6},{8,9},{9,8},{10,11... | collective-permute-start | bytes 786440 | tf_op jit(solution)/shard_map/ppermute | solution.py:34
  146.2 8.6 %collective-permute-start.23 = (bf16[1,16,2,1,16,256]{5,1,3,2,4,0:T(8,128)(2,1)}, bf16[1,16,2,1,16,256]{5,1,3,2,4,0:T(8,128)(2,1)}, u32[]{:S(2)}, u32[]{:S(2)}) collective-permute-start(bf16[1,16,2,1,16,256]{5,1,3,2,4,0:T(8,128)(2,1)} %get-tuple-element.10), channel_id=1, source_target_pairs={{0,3},{1,2},{2,1},{3,0},{4,7},{5,6},{6,5},{7,4},{8,11},{9,10},{10,... | collective-permute-start | bytes 786440 | tf_op jit(solution)/shard_map/ppermute | solution.py:34
  147.8 13.0 %collective-permute-start.22 = (bf16[1,16,2,1,16,256]{5,1,2,4,3,0:T(8,128)(2,1)}, bf16[1,16,2,1,16,256]{5,1,2,4,3,0:T(8,128)(2,1)}, u32[]{:S(2)}, u32[]{:S(2)}) collective-permute-start(bf16[1,16,2,1,16,256]{5,1,2,4,3,0:T(8,128)(2,1)} %get-tuple-element.11), channel_id=1, source_target_pairs={{0,2},{1,3},{2,0},{3,1},{4,6},{5,7},{6,4},{7,5},{8,10},{9,11},{10,... | collective-permute-start | bytes 786440 | tf_op jit(solution)/shard_map/ppermute | solution.py:34
  180.0 8.6 %collective-permute-start.9 = (bf16[1,16,2,1,16,256]{5,1,2,4,3,0:T(8,128)(2,1)}, bf16[1,16,2,1,16,256]{5,1,2,4,3,0:T(8,128)(2,1)}, u32[]{:S(2)}, u32[]{:S(2)}) collective-permute-start(bf16[1,16,2,1,16,256]{5,1,2,4,3,0:T(8,128)(2,1)} %get-tuple-element.25), channel_id=1, source_target_pairs={{0,1},{1,0},{2,3},{3,2},{4,5},{5,4},{6,7},{7,6},{8,9},{9,8},{10,11... | collective-permute-start | bytes 786440 | tf_op jit(solution)/shard_map/ppermute | solution.py:34
  180.0 8.6 %collective-permute-start.11 = (bf16[1,16,2,1,16,256]{5,1,3,2,4,0:T(8,128)(2,1)}, bf16[1,16,2,1,16,256]{5,1,3,2,4,0:T(8,128)(2,1)}, u32[]{:S(2)}, u32[]{:S(2)}) collective-permute-start(bf16[1,16,2,1,16,256]{5,1,3,2,4,0:T(8,128)(2,1)} %get-tuple-element.26), channel_id=1, source_target_pairs={{0,3},{1,2},{2,1},{3,0},{4,7},{5,6},{6,5},{7,4},{8,11},{9,10},{10,... | collective-permute-start | bytes 786440 | tf_op jit(solution)/shard_map/ppermute | solution.py:34
  181.6 13.0 %collective-permute-start.10 = (bf16[1,16,2,1,16,256]{5,1,2,4,3,0:T(8,128)(2,1)}, bf16[1,16,2,1,16,256]{5,1,2,4,3,0:T(8,128)(2,1)}, u32[]{:S(2)}, u32[]{:S(2)}) collective-permute-start(bf16[1,16,2,1,16,256]{5,1,2,4,3,0:T(8,128)(2,1)} %get-tuple-element.27), channel_id=1, source_target_pairs={{0,2},{1,3},{2,0},{3,1},{4,6},{5,7},{6,4},{7,5},{8,10},{9,11},{10,... | collective-permute-start | bytes 786440 | tf_op jit(solution)/shard_map/ppermute | solution.py:34
  199.5 2.8 %copy-start.12 = (f32[1,1,16,16384]{3,2,1,0:T(8,128)S(1)}, f32[1,1,16,16384]{3,2,1,0:T(8,128)}, u32[]{:S(2)}) copy-start(f32[1,1,16,16384]{3,2,1,0:T(8,128)} %stack.159) | copy-start | bytes 3145732
  (14 other events, 25.9 us)
Sparse Core Ops, SparseCore 0:
  10.2 51.7 all-gather.1
  177.3 86.8 reduce-scatter.1
